TPU v7x, 32 devices: a whole 2x2x4 slice. The times are simulated.
32 devices in a mesh: layer: 4 (over y, x), row: 2 (over core), col: 4 (over z).
Axes of the slice: x: 2, y: 2, z: 4, core: 2. Of those that a mesh axis runs over, the one named last changes fastest.
Arguments:
- blocks: bfloat16 [13, 512, 128, 128], P(None, ('row', 'col'), 'layer'), may hold values from -0.29882812 to 0.29882812
- presence: int32 [13, 512], P(None, ('row', 'col')), may hold values from 0 to 1, as said below
Outputs:
- purified: bfloat16 [13, 512, 128, 128], P(None, ('row', 'col'), 'layer')
Inputs may be any that keep to these rules, and one draw needn't show every extreme that they name: `presence`: the tile on offset 0 is present in every block row.
All inputs are finite; a program needn't handle non-finite values.
Results may differ from a plain program's by a relative error of at most 0.01.
Values may be sent and summed in bfloat16 or wider, within the bound.
A program may use at most 320 MiB of HBM per device.

v0:
```python
import jax
import jax.numpy as jnp
import numpy as np
from jax import lax
from jax.sharding import PartitionSpec as P

NBG = 512
BAND = 3
FAR = 160


def passed_along(block, axis, distance):
    devices = range(lax.axis_size(axis))
    route = [((i - distance) % len(devices), i) for i in devices]
    return lax.ppermute(block, axis, route)


def with_halo(block, sides, width):
    for axis, dim in sides:
        count = lax.axis_size(axis)
        forward = [(i, i + 1) for i in range(count - 1)]
        forward.append((count - 1, 0))
        backward = [(target, source) for source, target in forward]
        low = lax.ppermute(
            lax.slice_in_dim(block, block.shape[dim] - width, None, axis=dim), axis, forward
        )
        high = lax.ppermute(lax.slice_in_dim(block, 0, width, axis=dim), axis, backward)
        block = jnp.concatenate([low, block, high], axis=dim)
    return block


def offset_table():
    values = list(range(-BAND, BAND + 1))
    values = values + [FAR - 1, FAR, FAR + 1, -FAR - 1, -FAR, -FAR + 1]
    return [value % NBG for value in values]


def pair_table(offsets):
    by_target = []
    for target_index in range(len(offsets)):
        entries = []
        for left_index in range(len(offsets)):
            for right_index in range(len(offsets)):
                if (offsets[left_index] + offsets[right_index]) % NBG == offsets[target_index]:
                    entries.append((left_index, right_index))
        by_target.append(entries)
    return by_target


def fetch_far(source, offset, groups, local_rows):
    whole_steps, remainder = divmod(offset, local_rows)
    upper = passed_along(source[:, remainder:], ("row", "col"), -whole_steps % groups)
    if remainder == 0:
        return upper
    lower = passed_along(source[:, :remainder], ("row", "col"), (-whole_steps - 1) % groups)
    return jnp.concatenate([upper, lower], axis=1)


def per_device(blocks, presence):
    groups = lax.axis_size(("row", "col"))
    local_rows = blocks.shape[1]
    offsets = offset_table()
    by_target = pair_table(offsets)
    weight_mask = presence.astype(jnp.float32)[:, :, None, None]
    masked = blocks * presence.astype(jnp.bfloat16)[:, :, None, None]
    padded = with_halo(masked, ((("row", "col"), 1),), BAND)
    far_windows = {}
    for left_index in range(2 * BAND + 1, len(offsets)):
        needed = sorted(
            set(
                (
                    entry[1]
                    for target_list in by_target
                    for entry in target_list
                    if entry[0] == left_index
                )
            )
        )
        picked = jnp.take(masked, np.array(needed), axis=0)
        far_windows[left_index] = (
            fetch_far(picked, offsets[left_index], groups, local_rows),
            needed,
        )

    def right_piece(left_index, right_index):
        if left_index <= 2 * BAND:
            return padded[right_index, left_index : left_index + local_rows]
        window, needed = far_windows[left_index]
        return window[needed.index(right_index)]

    def product(left_tiles):
        totals = []
        for target_index in range(len(offsets)):
            pairs = by_target[target_index]
            lefts = jnp.concatenate(
                [left_tiles[left_index] for left_index, right_index in pairs], axis=2
            )
            rights = jnp.concatenate(
                [right_piece(left_index, right_index) for left_index, right_index in pairs], axis=1
            )
            totals.append(
                jnp.einsum("ixk,iky->ixy", lefts, rights, preferred_element_type=jnp.float32)
            )
        return jnp.stack(totals)

    left_first = lax.all_to_all(masked, "layer", split_axis=3, concat_axis=2, tiled=True)
    second = (
        lax.psum_scatter(product(left_first), "layer", scatter_dimension=2, tiled=True)
        * weight_mask
    ).astype(jnp.bfloat16)
    left_second = lax.all_to_all(second, "layer", split_axis=3, concat_axis=2, tiled=True)
    third = (
        lax.psum_scatter(
            product(left_second).astype(jnp.bfloat16), "layer", scatter_dimension=2, tiled=True
        ).astype(jnp.float32)
        * weight_mask
    )
    return (3.0 * second.astype(jnp.float32) - 2.0 * third).astype(jnp.bfloat16)


def solution(mesh):
    placed = (P(None, ("row", "col"), "layer", None), P(None, ("row", "col")))
    return jax.shard_map(
        per_device,
        mesh=mesh,
        in_specs=placed,
        out_specs=P(None, ("row", "col"), "layer", None),
        check_vma=False,
    )
```

profile of v0, /device:TPU:0, one launch (start us, length us, event | category | flops | bytes accessed | tf_op | source)
XLA Modules:
  0.0 2231.8 jit_solution(13494582447131702137)
XLA Ops:
  14.5 24.0 %copy.159 = bf16[13,64,32,128]{1,2,0,3:T(8,128)(2,1)} copy(bf16[13,64,32,128]{3,2,1,0:T(8,128)(2,1)} %broadcast_multiply_fusion) | data formatting | bytes 13631488 | tf_op jit(solution)/shard_map/mul | solution.py:65
  38.5 13.8 reshape.119
  134.3 111.9 %collective-permute-done.10 = bf16[6,31,32,128]{3,2,1,0:T(8,128)(2,1)} collective-permute-done((bf16[6,31,32,128]{3,2,1,0:T(8,128)(2,1)}, bf16[6,31,32,128]{3,2,1,0:T(8,128)(2,1)}, u32[]{:S(2)}, u32[]{:S(2)}) %collective-permute-start.10) | collective-permute-done | bytes 1523744 | tf_op jit(solution)/shard_map/ppermute | solution.py:15
  246.2 32.9 %collective-permute-start.4 = (bf16[6,33,32,128]{3,2,1,0:T(8,128)(2,1)S(1)}, bf16[6,33,32,128]{3,2,1,0:T(8,128)(2,1)S(1)}, u32[]{:S(2)}, u32[]{:S(2)}) collective-permute-start(bf16[6,33,32,128]{3,2,1,0:T(8,128)(2,1)S(1)} %copy-done.32), channel_id=1, source_target_pairs={{5,0},{6,1},{7,2},{0,3},{1,4},{2,5},{3,6},{4,7},{13,8},{14,9},{15,... | collective-permute-start | bytes 4866056 | tf_op jit(solution)/shard_map/ppermute | solution.py:15
  294.4 120.7 %collective-permute-start.2 = (bf16[6,33,32,128]{3,2,1,0:T(8,128)(2,1)S(1)}, bf16[6,33,32,128]{3,2,1,0:T(8,128)(2,1)}, u32[]{:S(2)}, u32[]{:S(2)}) collective-permute-start(bf16[6,33,32,128]{3,2,1,0:T(8,128)(2,1)S(1)} %slice.876), channel_id=1, source_target_pairs={{2,0},{3,1},{4,2},{5,3},{6,4},{7,5},{0,6},{1,7},{10,8},{11,9},{12,... | collective-permute-start | bytes 4866056 | tf_op jit(solution)/shard_map/ppermute | solution.py:15
  417.0 97.6 %collective-permute-done.9 = bf16[6,32,32,128]{3,2,1,0:T(8,128)(2,1)S(1)} collective-permute-done((bf16[6,32,32,128]{3,2,1,0:T(8,128)(2,1)S(1)}, bf16[6,32,32,128]{3,2,1,0:T(8,128)(2,1)S(1)}, u32[]{:S(2)}, u32[]{:S(2)}) %collective-permute-start.9) | collective-permute-done | bytes 1572896 | tf_op jit(solution)/shard_map/ppermute | solution.py:15
  523.1 93.8 %collective-permute-done.5 = bf16[6,31,32,128]{3,2,1,0:T(8,128)(2,1)} collective-permute-done((bf16[6,31,32,128]{3,2,1,0:T(8,128)(2,1)}, bf16[6,31,32,128]{3,2,1,0:T(8,128)(2,1)}, u32[]{:S(2)}, u32[]{:S(2)}) %collective-permute-start.5) | collective-permute-done | bytes 1523744 | tf_op jit(solution)/shard_map/ppermute | solution.py:15
  618.6 33.1 %collective-permute-done.2 = bf16[6,33,32,128]{3,2,1,0:T(8,128)(2,1)} collective-permute-done((bf16[6,33,32,128]{3,2,1,0:T(8,128)(2,1)S(1)}, bf16[6,33,32,128]{3,2,1,0:T(8,128)(2,1)}, u32[]{:S(2)}, u32[]{:S(2)}) %collective-permute-start.2) | collective-permute-done | bytes 1622048 | tf_op jit(solution)/shard_map/ppermute | solution.py:15
  655.7 30.6 %collective-permute-done.13 = bf16[6,33,32,128]{3,2,1,0:T(8,128)(2,1)S(1)} collective-permute-done((bf16[6,33,32,128]{3,2,1,0:T(8,128)(2,1)S(1)}, bf16[6,33,32,128]{3,2,1,0:T(8,128)(2,1)S(1)}, u32[]{:S(2)}, u32[]{:S(2)}) %collective-permute-start.13) | collective-permute-done | bytes 1622048 | tf_op jit(solution)/shard_map/ppermute | solution.py:15
  701.1 13.7 reshape.120
  795.0 15.4 concatenate.198
  810.4 21.3 concatenate.203
  831.7 26.5 %concatenate.207 = bf16[64,128,416]{2,1,0:T(8,128)(2,1)} concatenate(bf16[64,128,32]{2,1,0:T(8,128)(2,1)} %bitcast.600, bf16[64,128,32]{2,1,0:T(8,128)(2,1)} %bitcast.496, bf16[64,128,32]{2,1,0:T(8,128)(2,1)} %bitcast.472, bf16[64,128,32]{2,1,0:T(8,128)(2,1)S(1)} %bitcast.429, bf16[64,128,32]{2,1,0:T(8,128)(2,1)} %bitcast.452, bf16[64,128,32]{2,1,0:T(8,128)(2,1)} %bitcast.488, ...), dimensions={2} | concatenate | bytes 13631488 | tf_op jit(solution)/shard_map/concatenate | solution.py:95
  858.2 21.3 concatenate.211
  879.5 15.5 concatenate.213
  895.0 13.6 concatenate.217
  908.6 13.2 concatenate.219
  948.1 13.2 concatenate.225
  961.3 13.3 concatenate.227
  1048.6 457.3 %reduce-scatter.3.cloned.1.call-done = f32[13,64,32,128]{3,2,1,0:T(8,128)} async-done(((f32[13,64,128,128]{3,2,1,0:T(8,128)}), f32[13,64,32,128]{3,2,1,0:T(8,128)}) %reduce-scatter.3.cloned.1.call-update) | async-done | bytes 13631504 | tf_op jit(solution)/shard_map/reduce_scatter | solution.py:108
  1514.0 24.0 %copy.185 = bf16[13,64,32,128]{1,2,0,3:T(8,128)(2,1)} copy(bf16[13,64,32,128]{3,2,1,0:T(8,128)(2,1)} %multiply_convert_fusion) | data formatting | bytes 13631488 | tf_op jit(solution)/shard_map/convert_element_type | solution.py:110
  1538.1 13.8 reshape.121
  1551.9 83.3 %all_to_all.30 = bf16[4,2,425984]{2,1,0:T(2,128)(2,1)} all-to-all(bf16[4,2,425984]{2,1,0:T(2,128)(2,1)} %reshape.121), channel_id=1, replica_groups=mesh['layer'=4,'row'=2,'col'=4] {'layer'}, dimensions={0} | all-to-all | bytes 13631488 | tf_op jit(solution)/shard_map/all_to_all | solution.py:111
  1635.2 13.5 reshape.122
  1736.3 15.4 concatenate.230
  1751.7 21.3 concatenate.231
  1773.0 26.5 %concatenate.232 = bf16[64,128,416]{2,1,0:T(8,128)(2,1)} concatenate(bf16[64,128,32]{2,1,0:T(8,128)(2,1)} %bitcast.605, bf16[64,128,32]{2,1,0:T(8,128)(2,1)} %bitcast.504, bf16[64,128,32]{2,1,0:T(8,128)(2,1)} %bitcast.463, bf16[64,128,32]{2,1,0:T(8,128)(2,1)S(1)} %bitcast.417, bf16[64,128,32]{2,1,0:T(8,128)(2,1)} %bitcast.442, bf16[64,128,32]{2,1,0:T(8,128)(2,1)} %bitcast.481, ...), dimensions={2} | concatenate | bytes 13631488 | tf_op jit(solution)/shard_map/concatenate | solution.py:95
  1799.5 21.3 concatenate.233
  1820.8 15.5 concatenate.234
  1849.5 13.2 concatenate.237
  1902.2 13.4 concatenate.241
  1975.5 238.3 %reduce-scatter.5.cloned.1.call-done = bf16[13,64,32,128]{3,2,1,0:T(8,128)(2,1)} async-done(((bf16[13,64,128,128]{3,2,1,0:T(8,128)(2,1)}), bf16[13,64,32,128]{3,2,1,0:T(8,128)(2,1)}) %reduce-scatter.5.cloned.1.call-update) | async-done | bytes 6815760 | tf_op jit(solution)/shard_map/reduce_scatter | solution.py:113
  (288 shorter events, 535.1 us)
Async XLA Ops:
  52.3 12.0 copy-start.58
  52.3 12.0 copy-start.59
  52.3 648.8 %all-to-all-start = ((bf16[4,2,425984]{2,1,0:T(2,128)(2,1)}), bf16[4,2,425984]{2,1,0:T(2,128)(2,1)}, u32[]{:S(2)}, u32[]{:S(2)}) async-start(bf16[4,2,425984]{2,1,0:T(2,128)(2,1)} %reshape.119), calls=%async_computation | async-start | bytes 13631488 | tf_op jit(solution)/shard_map/all_to_all | solution.py:106
  57.7 1448.2 %reduce-scatter.3.cloned.1.call-start = ((), (), s32[]{:S(2)}) async-start(), calls=%async_computation.4 | async-start | bytes 68157440 | tf_op jit(solution)/shard_map/reduce_scatter | solution.py:108
  59.7 67.6 %collective-permute-start.1 = (bf16[13,3,32,128]{3,2,1,0:T(8,128)(2,1)}, bf16[13,3,32,128]{3,2,1,0:T(8,128)(2,1)S(1)}, u32[]{:S(2)}, u32[]{:S(2)}) collective-permute-start(bf16[13,3,32,128]{3,2,1,0:T(8,128)(2,1)} %get-tuple-element.88), channel_id=1, source_target_pairs={{1,0},{2,1},{3,2},{4,3},{5,4},{6,5},{7,6},{0,7},{9,8},{10,9},{11,1... | collective-permute-start | bytes 958472 | tf_op jit(solution)/shard_map/ppermute | solution.py:27
  64.3 54.9 %collective-permute-start = (bf16[13,3,32,128]{3,2,1,0:T(8,128)(2,1)}, bf16[13,3,32,128]{3,2,1,0:T(8,128)(2,1)}, u32[]{:S(2)}, u32[]{:S(2)}) collective-permute-start(bf16[13,3,32,128]{3,2,1,0:T(8,128)(2,1)} %get-tuple-element.89), channel_id=1, source_target_pairs={{0,1},{1,2},{2,3},{3,4},{4,5},{5,6},{6,7},{7,0},{8,9},{9,10},{10,1... | collective-permute-start | bytes 958472 | tf_op jit(solution)/shard_map/ppermute | solution.py:24
  70.8 216.8 %collective-permute-start.6 = (bf16[6,32,32,128]{3,2,1,0:T(8,128)(2,1)}, bf16[6,32,32,128]{3,2,1,0:T(8,128)(2,1)}, u32[]{:S(2)}, u32[]{:S(2)}) collective-permute-start(bf16[6,32,32,128]{3,2,1,0:T(8,128)(2,1)} %get-tuple-element.129), channel_id=1, source_target_pairs={{2,0},{3,1},{4,2},{5,3},{6,4},{7,5},{0,6},{1,7},{10,8},{11,9},{12,... | collective-permute-start | bytes 4718600 | tf_op jit(solution)/shard_map/ppermute | solution.py:15
  75.3 9.9 copy-start.30
  77.1 169.1 %collective-permute-start.10 = (bf16[6,31,32,128]{3,2,1,0:T(8,128)(2,1)}, bf16[6,31,32,128]{3,2,1,0:T(8,128)(2,1)}, u32[]{:S(2)}, u32[]{:S(2)}) collective-permute-start(bf16[6,31,32,128]{3,2,1,0:T(8,128)(2,1)} %slice.922), channel_id=1, source_target_pairs={{2,0},{3,1},{4,2},{5,3},{6,4},{7,5},{0,6},{1,7},{10,8},{11,9},{12,... | collective-permute-start | bytes 4571144 | tf_op jit(solution)/shard_map/ppermute | solution.py:15
  88.0 191.1 %collective-permute-start.12 = (bf16[6,31,32,128]{3,2,1,0:T(8,128)(2,1)}, bf16[6,31,32,128]{3,2,1,0:T(8,128)(2,1)}, u32[]{:S(2)}, u32[]{:S(2)}) collective-permute-start(bf16[6,31,32,128]{3,2,1,0:T(8,128)(2,1)} %slice.927), channel_id=1, source_target_pairs={{5,0},{6,1},{7,2},{0,3},{1,4},{2,5},{3,6},{4,7},{13,8},{14,9},{15,... | collective-permute-start | bytes 4571144 | tf_op jit(solution)/shard_map/ppermute | solution.py:15
  105.4 13.0 slice-start
  119.2 175.2 %collective-permute-start.7 = (bf16[6,32,32,128]{3,2,1,0:T(8,128)(2,1)S(1)}, bf16[6,32,32,128]{3,2,1,0:T(8,128)(2,1)S(1)}, u32[]{:S(2)}, u32[]{:S(2)}) collective-permute-start(bf16[6,32,32,128]{3,2,1,0:T(8,128)(2,1)S(1)} %copy-done.39), channel_id=1, source_target_pairs={{3,0},{4,1},{5,2},{6,3},{7,4},{0,5},{1,6},{2,7},{11,8},{12,9},{13,... | collective-permute-start | bytes 4718600 | tf_op jit(solution)/shard_map/ppermute | solution.py:15
  127.3 287.8 %collective-permute-start.8 = (bf16[6,32,32,128]{3,2,1,0:T(8,128)(2,1)S(1)}, bf16[6,32,32,128]{3,2,1,0:T(8,128)(2,1)S(1)}, u32[]{:S(2)}, u32[]{:S(2)}) collective-permute-start(bf16[6,32,32,128]{3,2,1,0:T(8,128)(2,1)S(1)} %copy-done.41), channel_id=1, source_target_pairs={{5,0},{6,1},{7,2},{0,3},{1,4},{2,5},{3,6},{4,7},{13,8},{14,9},{15,... | collective-permute-start | bytes 4718600 | tf_op jit(solution)/shard_map/ppermute | solution.py:15
  131.2 115.0 %copy-start.32 = (bf16[6,33,32,128]{3,2,1,0:T(8,128)(2,1)S(1)}, bf16[6,33,32,128]{3,2,1,0:T(8,128)(2,1)}, u32[]{:S(2)}) copy-start(bf16[6,33,32,128]{3,2,1,0:T(8,128)(2,1)} %slice.879) | copy-start | bytes 4866052
  131.2 147.9 %copy-start.40 = (bf16[6,32,32,128]{3,2,1,0:T(8,128)(2,1)S(1)}, bf16[6,32,32,128]{3,2,1,0:T(8,128)(2,1)}, u32[]{:S(2)}) copy-start(bf16[6,32,32,128]{3,2,1,0:T(8,128)(2,1)} %get-tuple-element.126) | copy-start | bytes 4718596
  246.2 269.4 %collective-permute-start.4 = (bf16[6,33,32,128]{3,2,1,0:T(8,128)(2,1)S(1)}, bf16[6,33,32,128]{3,2,1,0:T(8,128)(2,1)S(1)}, u32[]{:S(2)}, u32[]{:S(2)}) collective-permute-start(bf16[6,33,32,128]{3,2,1,0:T(8,128)(2,1)S(1)} %copy-done.32), channel_id=1, source_target_pairs={{5,0},{6,1},{7,2},{0,3},{1,4},{2,5},{3,6},{4,7},{13,8},{14,9},{15,... | collective-permute-start | bytes 4866056 | tf_op jit(solution)/shard_map/ppermute | solution.py:15
  279.1 235.5 %collective-permute-start.9 = (bf16[6,32,32,128]{3,2,1,0:T(8,128)(2,1)S(1)}, bf16[6,32,32,128]{3,2,1,0:T(8,128)(2,1)S(1)}, u32[]{:S(2)}, u32[]{:S(2)}) collective-permute-start(bf16[6,32,32,128]{3,2,1,0:T(8,128)(2,1)S(1)} %copy-done.40), channel_id=1, source_target_pairs={{6,0},{7,1},{0,2},{1,3},{2,4},{3,5},{4,6},{5,7},{14,8},{15,9},{8,1... | collective-permute-start | bytes 4718600 | tf_op jit(solution)/shard_map/ppermute | solution.py:15
  287.6 329.3 %collective-permute-start.5 = (bf16[6,31,32,128]{3,2,1,0:T(8,128)(2,1)}, bf16[6,31,32,128]{3,2,1,0:T(8,128)(2,1)}, u32[]{:S(2)}, u32[]{:S(2)}) collective-permute-start(bf16[6,31,32,128]{3,2,1,0:T(8,128)(2,1)} %slice.880), channel_id=1, source_target_pairs={{6,0},{7,1},{0,2},{1,3},{2,4},{3,5},{4,6},{5,7},{14,8},{15,9},{8,1... | collective-permute-start | bytes 4571144 | tf_op jit(solution)/shard_map/ppermute | solution.py:15
  294.4 122.6 %copy-start.33 = (bf16[6,32,32,128]{3,2,1,0:T(8,128)(2,1)}, bf16[6,32,32,128]{3,2,1,0:T(8,128)(2,1)S(1)}, u32[]{:S(2)}) copy-start(bf16[6,32,32,128]{3,2,1,0:T(8,128)(2,1)S(1)} %collective-permute-done.7) | copy-start | bytes 4718596
  294.4 357.3 %collective-permute-start.2 = (bf16[6,33,32,128]{3,2,1,0:T(8,128)(2,1)S(1)}, bf16[6,33,32,128]{3,2,1,0:T(8,128)(2,1)}, u32[]{:S(2)}, u32[]{:S(2)}) collective-permute-start(bf16[6,33,32,128]{3,2,1,0:T(8,128)(2,1)S(1)} %slice.876), channel_id=1, source_target_pairs={{2,0},{3,1},{4,2},{5,3},{6,4},{7,5},{0,6},{1,7},{10,8},{11,9},{12,... | collective-permute-start | bytes 4866056 | tf_op jit(solution)/shard_map/ppermute | solution.py:15
  415.1 238.4 %collective-permute-start.3 = (bf16[6,31,32,128]{3,2,1,0:T(8,128)(2,1)}, bf16[6,31,32,128]{3,2,1,0:T(8,128)(2,1)}, u32[]{:S(2)}, u32[]{:S(2)}) collective-permute-start(bf16[6,31,32,128]{3,2,1,0:T(8,128)(2,1)} %slice.877), channel_id=1, source_target_pairs={{3,0},{4,1},{5,2},{6,3},{7,4},{0,5},{1,6},{2,7},{11,8},{12,9},{13,... | collective-permute-start | bytes 4571144 | tf_op jit(solution)/shard_map/ppermute | solution.py:15
  514.6 140.6 %collective-permute-start.11 = (bf16[6,33,32,128]{3,2,1,0:T(8,128)(2,1)S(1)}, bf16[6,33,32,128]{3,2,1,0:T(8,128)(2,1)S(1)}, u32[]{:S(2)}, u32[]{:S(2)}) collective-permute-start(bf16[6,33,32,128]{3,2,1,0:T(8,128)(2,1)S(1)} %slice.923), channel_id=1, source_target_pairs={{3,0},{4,1},{5,2},{6,3},{7,4},{0,5},{1,6},{2,7},{11,8},{12,9},{13,... | collective-permute-start | bytes 4866056 | tf_op jit(solution)/shard_map/ppermute | solution.py:15
  515.6 170.7 %collective-permute-start.13 = (bf16[6,33,32,128]{3,2,1,0:T(8,128)(2,1)S(1)}, bf16[6,33,32,128]{3,2,1,0:T(8,128)(2,1)S(1)}, u32[]{:S(2)}, u32[]{:S(2)}) collective-permute-start(bf16[6,33,32,128]{3,2,1,0:T(8,128)(2,1)S(1)} %slice.928), channel_id=1, source_target_pairs={{6,0},{7,1},{0,2},{1,3},{2,4},{3,5},{4,6},{5,7},{14,8},{15,9},{8,1... | collective-permute-start | bytes 4866056 | tf_op jit(solution)/shard_map/ppermute | solution.py:15
  961.3 13.3 copy-start.50
  961.3 13.3 copy-start.51
  982.5 13.7 slice-start.2
  988.0 15.7 slice-start.4
  1048.5 457.4 %copy-start.52 = (f32[13,64]{1,0:T(8,128)S(1)}, f32[13,64]{1,0:T(8,128)}, u32[]{:S(2)}) copy-start(f32[13,64]{1,0:T(8,128)} %get-tuple-element.130) | copy-start | bytes 9988
  1048.5 1165.4 %reduce-scatter.5.cloned.1.call-start = ((), (), s32[]{:S(2)}) async-start(), calls=%async_computation.5 | async-start | bytes 34078720 | tf_op jit(solution)/shard_map/reduce_scatter | solution.py:113
  1915.6 13.6 slice-start.8
  1921.7 14.5 slice-start.6
  1975.5 238.4 %copy-start.53 = (f32[13,64]{1,0:T(8,128)S(1)}, f32[13,64]{1,0:T(8,128)}, u32[]{:S(2)}) copy-start(f32[13,64]{1,0:T(8,128)} %get-tuple-element.130) | copy-start | bytes 9988
  (55 other events, 260.7 us)
Sparse Core Ops, SparseCore 0:
  1048.6 457.2 reduce-scatter.2
  1975.7 238.1 reduce-scatter.4
where the time goes:
time: 2250 us; the launch traced here: 2230 us
  waiting for transfers between devices  1060 us (47%)
  local copies, waits for them, and re-layouts  707 us (31%)
  starting transfers between devices  179 us (8%)
  matrix products  136 us (6%)
  blocking collectives  83.3 us (4%)
  other arithmetic  49.6 us (2%)
    reduce_scatter x1, waiting for transfers between devices, per_device(): lax.psum_scatter(product(left_first), 'layer', scatter_dimension=2, tiled...  457 us
    ppermute x12, waiting for transfers between devices, passed_along(): return lax.ppermute(block, axis, route)  367 us
    concatenate x22, local copies, waits for them, and re-layouts, product(): jnp.concatenate([left_tiles[left_index] for left_index, right_index in pa...  359 us
    reduce_scatter x1, waiting for transfers between devices, per_device(): lax.psum_scatter(product(left_second).astype(jnp.bfloat16), 'layer', scat...  238 us
    ppermute x12, starting transfers between devices, passed_along(): return lax.ppermute(block, axis, route)  169 us
    dot_general x26, matrix products, product(): jnp.einsum('ixk,iky->ixy', lefts, rights, preferred_element_type=jnp.floa...  136 us
    slice x28, local copies, waits for them, and re-layouts, product(): left_tiles[left_index]  134 us
    all_to_all x1, blocking collectives, per_device(): lax.all_to_all(second, 'layer', split_axis=3, concat_axis=2, tiled=True)  83.3 us
  transfers between devices with their start and end apart: 17, of which 7 were waited for; matrix products, arithmetic and copies ran while one was open for 5% of the time, Pallas kernels for 0%

commit v1 on v0

--- a/solution.py
+++ b/solution.py
@@ -108,7 +108,15 @@
         lax.psum_scatter(product(left_first), "layer", scatter_dimension=2, tiled=True)
         * weight_mask
     ).astype(jnp.bfloat16)
-    left_second = lax.all_to_all(second, "layer", split_axis=3, concat_axis=2, tiled=True)
+    left_second = jnp.concatenate(
+        jax.lax.all_to_all(
+            jnp.stack(jnp.split(second, jax.lax.axis_size("layer"), 3), 0),
+            split_axis=0,
+            concat_axis=0,
+            axis_name="layer",
+        ),
+        2,
+    )
     third = (
         lax.psum_scatter(
             product(left_second).astype(jnp.bfloat16), "layer", scatter_dimension=2, tiled=True

time: 2250 us -> 2150 us (0.956)
  local copies, waits for them, and re-layouts: 707 us -> 587 us
    concatenate x22 -> x13, local copies, waits for them, and re-layouts: 359 us -> 184 us  [product(): jnp.concatenate([left_tiles[left_index] for left_index, right_index in pa...]
    squeeze x0 -> x20, local copies, waits for them, and re-layouts: none -> 75.1 us  [product(): left_tiles[left_index]]
    slice x28 -> x15, local copies, waits for them, and re-layouts: 134 us -> 71.3 us  [product(): left_tiles[left_index]]
    another operation x0 -> x2, local copies, waits for them, and re-layouts: none -> 45.1 us  [per_device(): jnp.stack(jnp.split(second, jax.lax.axis_size('layer'), 3), 0)]
    unnamed x155 -> x199, local copies, waits for them, and re-layouts: 79.8 us -> 107 us
    convert_element_type x1 -> x0, local copies, waits for them, and re-layouts: 24 us -> none  [per_device(): second = (lax.psum_scatter(product(left_first), 'layer', scatter_dimensio...]
where the time goes in v1:
time: 2150 us; the launch traced here: 2140 us
  waiting for transfers between devices  1060 us (49%)
  local copies, waits for them, and re-layouts  587 us (27%)
  starting transfers between devices  179 us (8%)
  matrix products  142 us (7%)
  blocking collectives  83.2 us (4%)
  other arithmetic  66.4 us (3%)
    reduce_scatter x1, waiting for transfers between devices, per_device(): lax.psum_scatter(product(left_first), 'layer', scatter_dimension=2, tiled...  457 us
    ppermute x12, waiting for transfers between devices, passed_along(): return lax.ppermute(block, axis, route)  367 us
    reduce_scatter x1, waiting for transfers between devices, per_device(): lax.psum_scatter(product(left_second).astype(jnp.bfloat16), 'layer', scat...  238 us
    concatenate x13, local copies, waits for them, and re-layouts, product(): jnp.concatenate([left_tiles[left_index] for left_index, right_index in pa...  184 us
    ppermute x12, starting transfers between devices, passed_along(): return lax.ppermute(block, axis, route)  169 us
    dot_general x26, matrix products, product(): jnp.einsum('ixk,iky->ixy', lefts, rights, preferred_element_type=jnp.floa...  142 us
    unnamed x199, local copies, waits for them, and re-layouts  107 us
    all_to_all x1, blocking collectives, per_device(): jax.lax.all_to_all(jnp.stack(jnp.split(second, jax.lax.axis_size('layer')...  83.2 us
  transfers between devices with their start and end apart: 17, of which 7 were waited for; matrix products, arithmetic and copies ran while one was open for 5% of the time, Pallas kernels for 0%

profile of v1, /device:TPU:0, one launch (start us, length us, event | category | flops | bytes accessed | tf_op | source)
XLA Modules:
  0.0 2135.4 jit_solution(11657083775965040314)
XLA Ops:
  14.5 24.0 %copy.291 = bf16[13,64,32,128]{1,2,0,3:T(8,128)(2,1)} copy(bf16[13,64,32,128]{3,2,1,0:T(8,128)(2,1)} %broadcast_multiply_fusion) | data formatting | bytes 13631488 | tf_op jit(solution)/shard_map/mul | solution.py:65
  38.5 13.8 reshape.124
  134.3 112.0 %collective-permute-done.10 = bf16[6,31,32,128]{3,2,1,0:T(8,128)(2,1)} collective-permute-done((bf16[6,31,32,128]{3,2,1,0:T(8,128)(2,1)}, bf16[6,31,32,128]{3,2,1,0:T(8,128)(2,1)}, u32[]{:S(2)}, u32[]{:S(2)}) %collective-permute-start.10) | collective-permute-done | bytes 1523744 | tf_op jit(solution)/shard_map/ppermute | solution.py:15
  246.3 32.9 %collective-permute-start.4 = (bf16[6,33,32,128]{3,2,1,0:T(8,128)(2,1)S(1)}, bf16[6,33,32,128]{3,2,1,0:T(8,128)(2,1)S(1)}, u32[]{:S(2)}, u32[]{:S(2)}) collective-permute-start(bf16[6,33,32,128]{3,2,1,0:T(8,128)(2,1)S(1)} %copy-done.52), channel_id=1, source_target_pairs={{5,0},{6,1},{7,2},{0,3},{1,4},{2,5},{3,6},{4,7},{13,8},{14,9},{15,... | collective-permute-start | bytes 4866056 | tf_op jit(solution)/shard_map/ppermute | solution.py:15
  294.4 120.7 %collective-permute-start.2 = (bf16[6,33,32,128]{3,2,1,0:T(8,128)(2,1)S(1)}, bf16[6,33,32,128]{3,2,1,0:T(8,128)(2,1)}, u32[]{:S(2)}, u32[]{:S(2)}) collective-permute-start(bf16[6,33,32,128]{3,2,1,0:T(8,128)(2,1)S(1)} %slice.876), channel_id=1, source_target_pairs={{2,0},{3,1},{4,2},{5,3},{6,4},{7,5},{0,6},{1,7},{10,8},{11,9},{12,... | collective-permute-start | bytes 4866056 | tf_op jit(solution)/shard_map/ppermute | solution.py:15
  417.0 97.6 %collective-permute-done.9 = bf16[6,32,32,128]{3,2,1,0:T(8,128)(2,1)S(1)} collective-permute-done((bf16[6,32,32,128]{3,2,1,0:T(8,128)(2,1)S(1)}, bf16[6,32,32,128]{3,2,1,0:T(8,128)(2,1)S(1)}, u32[]{:S(2)}, u32[]{:S(2)}) %collective-permute-start.9) | collective-permute-done | bytes 1572896 | tf_op jit(solution)/shard_map/ppermute | solution.py:15
  523.1 93.9 %collective-permute-done.5 = bf16[6,31,32,128]{3,2,1,0:T(8,128)(2,1)} collective-permute-done((bf16[6,31,32,128]{3,2,1,0:T(8,128)(2,1)}, bf16[6,31,32,128]{3,2,1,0:T(8,128)(2,1)}, u32[]{:S(2)}, u32[]{:S(2)}) %collective-permute-start.5) | collective-permute-done | bytes 1523744 | tf_op jit(solution)/shard_map/ppermute | solution.py:15
  618.7 33.1 %collective-permute-done.2 = bf16[6,33,32,128]{3,2,1,0:T(8,128)(2,1)} collective-permute-done((bf16[6,33,32,128]{3,2,1,0:T(8,128)(2,1)S(1)}, bf16[6,33,32,128]{3,2,1,0:T(8,128)(2,1)}, u32[]{:S(2)}, u32[]{:S(2)}) %collective-permute-start.2) | collective-permute-done | bytes 1622048 | tf_op jit(solution)/shard_map/ppermute | solution.py:15
  655.7 30.6 %collective-permute-done.13 = bf16[6,33,32,128]{3,2,1,0:T(8,128)(2,1)S(1)} collective-permute-done((bf16[6,33,32,128]{3,2,1,0:T(8,128)(2,1)S(1)}, bf16[6,33,32,128]{3,2,1,0:T(8,128)(2,1)S(1)}, u32[]{:S(2)}, u32[]{:S(2)}) %collective-permute-start.13) | collective-permute-done | bytes 1622048 | tf_op jit(solution)/shard_map/ppermute | solution.py:15
  701.1 13.9 reshape.125
  715.0 13.1 copy.292
  795.2 15.5 concatenate.198
  810.6 21.3 concatenate.203
  831.9 26.5 %concatenate.207 = bf16[64,128,416]{2,1,0:T(8,128)(2,1)} concatenate(bf16[64,128,32]{2,1,0:T(8,128)(2,1)} %bitcast.519, bf16[64,128,32]{2,1,0:T(8,128)(2,1)} %bitcast.464, bf16[64,128,32]{2,1,0:T(8,128)(2,1)} %bitcast.447, bf16[64,128,32]{2,1,0:T(8,128)(2,1)S(1)} %bitcast.424, bf16[64,128,32]{2,1,0:T(8,128)(2,1)} %bitcast.437, bf16[64,128,32]{2,1,0:T(8,128)(2,1)} %bitcast.456, ...), dimensions={2} | concatenate | bytes 13631488 | tf_op jit(solution)/shard_map/concatenate | solution.py:95
  858.5 21.3 concatenate.211
  879.7 15.5 concatenate.213
  895.3 13.6 concatenate.217
  908.8 13.2 concatenate.219
  922.0 13.2 concatenate.221
  935.3 13.2 concatenate.223
  948.5 13.2 concatenate.225
  961.7 13.3 concatenate.227
  1049.2 457.4 %reduce-scatter.3.cloned.1.call-done = f32[13,64,32,128]{3,2,1,0:T(8,128)} async-done(((f32[13,64,128,128]{3,2,1,0:T(8,128)}), f32[13,64,32,128]{3,2,1,0:T(8,128)}) %reduce-scatter.3.cloned.1.call-update) | async-done | bytes 13631504 | tf_op jit(solution)/shard_map/reduce_scatter | solution.py:108
  1512.5 11.3 slice_bitcast_fusion.3
  1523.9 19.0 pad_maximum_fusion
  1542.9 33.8 %copy.317 = bf16[4,13,64,32,32]{2,4,3,1,0:T(8,128)(2,1)} copy(bf16[4,13,64,32,32]{4,3,2,1,0:T(8,128)(2,1)} %pad_maximum_fusion) | data formatting | bytes 13631488 | tf_op jit(solution)/shard_map/stack | solution.py:113
  1576.7 13.8 reshape.126
  1590.5 83.2 %all_to_all.20 = bf16[4,2,425984]{2,1,0:T(2,128)(2,1)} all-to-all(bf16[4,2,425984]{2,1,0:T(2,128)(2,1)} %reshape.126), channel_id=1, replica_groups=mesh['layer'=4,'row'=2,'col'=4] {'layer'}, dimensions={0} | all-to-all | bytes 13631488 | tf_op jit(solution)/shard_map/all_to_all | solution.py:112
  1673.8 13.5 reshape.127
  1828.9 8.9 bitcast_dynamic-update-slice_fusion.22
  1879.4 238.3 %reduce-scatter.5.cloned.1.call-done = bf16[13,64,32,128]{3,2,1,0:T(8,128)(2,1)} async-done(((bf16[13,64,128,128]{3,2,1,0:T(8,128)(2,1)}), bf16[13,64,32,128]{3,2,1,0:T(8,128)(2,1)}) %reduce-scatter.5.cloned.1.call-update) | async-done | bytes 6815760 | tf_op jit(solution)/shard_map/reduce_scatter | solution.py:121
  2117.7 10.7 subtract_convert_fusion
  (330 shorter events, 465.7 us)
Async XLA Ops:
  52.3 12.0 copy-start.77
  52.3 12.0 copy-start.78
  52.3 648.9 %all-to-all-start = ((bf16[4,2,425984]{2,1,0:T(2,128)(2,1)}), bf16[4,2,425984]{2,1,0:T(2,128)(2,1)}, u32[]{:S(2)}, u32[]{:S(2)}) async-start(bf16[4,2,425984]{2,1,0:T(2,128)(2,1)} %reshape.124), calls=%async_computation | async-start | bytes 13631488 | tf_op jit(solution)/shard_map/all_to_all | solution.py:106
  57.7 1448.9 %reduce-scatter.3.cloned.1.call-start = ((), (), s32[]{:S(2)}) async-start(), calls=%async_computation.4 | async-start | bytes 68157440 | tf_op jit(solution)/shard_map/reduce_scatter | solution.py:108
  59.8 67.5 %collective-permute-start.1 = (bf16[13,3,32,128]{3,2,1,0:T(8,128)(2,1)}, bf16[13,3,32,128]{3,2,1,0:T(8,128)(2,1)S(1)}, u32[]{:S(2)}, u32[]{:S(2)}) collective-permute-start(bf16[13,3,32,128]{3,2,1,0:T(8,128)(2,1)} %get-tuple-element.92), channel_id=1, source_target_pairs={{1,0},{2,1},{3,2},{4,3},{5,4},{6,5},{7,6},{0,7},{9,8},{10,9},{11,1... | collective-permute-start | bytes 958472 | tf_op jit(solution)/shard_map/ppermute | solution.py:27
  64.3 54.9 %collective-permute-start = (bf16[13,3,32,128]{3,2,1,0:T(8,128)(2,1)}, bf16[13,3,32,128]{3,2,1,0:T(8,128)(2,1)}, u32[]{:S(2)}, u32[]{:S(2)}) collective-permute-start(bf16[13,3,32,128]{3,2,1,0:T(8,128)(2,1)} %get-tuple-element.93), channel_id=1, source_target_pairs={{0,1},{1,2},{2,3},{3,4},{4,5},{5,6},{6,7},{7,0},{8,9},{9,10},{10,1... | collective-permute-start | bytes 958472 | tf_op jit(solution)/shard_map/ppermute | solution.py:24
  70.8 216.7 %collective-permute-start.6 = (bf16[6,32,32,128]{3,2,1,0:T(8,128)(2,1)}, bf16[6,32,32,128]{3,2,1,0:T(8,128)(2,1)}, u32[]{:S(2)}, u32[]{:S(2)}) collective-permute-start(bf16[6,32,32,128]{3,2,1,0:T(8,128)(2,1)} %get-tuple-element.133), channel_id=1, source_target_pairs={{2,0},{3,1},{4,2},{5,3},{6,4},{7,5},{0,6},{1,7},{10,8},{11,9},{12,... | collective-permute-start | bytes 4718600 | tf_op jit(solution)/shard_map/ppermute | solution.py:15
  75.3 9.8 copy-start.25
  77.0 169.2 %collective-permute-start.10 = (bf16[6,31,32,128]{3,2,1,0:T(8,128)(2,1)}, bf16[6,31,32,128]{3,2,1,0:T(8,128)(2,1)}, u32[]{:S(2)}, u32[]{:S(2)}) collective-permute-start(bf16[6,31,32,128]{3,2,1,0:T(8,128)(2,1)} %slice.922), channel_id=1, source_target_pairs={{2,0},{3,1},{4,2},{5,3},{6,4},{7,5},{0,6},{1,7},{10,8},{11,9},{12,... | collective-permute-start | bytes 4571144 | tf_op jit(solution)/shard_map/ppermute | solution.py:15
  88.0 191.1 %collective-permute-start.12 = (bf16[6,31,32,128]{3,2,1,0:T(8,128)(2,1)}, bf16[6,31,32,128]{3,2,1,0:T(8,128)(2,1)}, u32[]{:S(2)}, u32[]{:S(2)}) collective-permute-start(bf16[6,31,32,128]{3,2,1,0:T(8,128)(2,1)} %slice.927), channel_id=1, source_target_pairs={{5,0},{6,1},{7,2},{0,3},{1,4},{2,5},{3,6},{4,7},{13,8},{14,9},{15,... | collective-permute-start | bytes 4571144 | tf_op jit(solution)/shard_map/ppermute | solution.py:15
  105.4 12.9 slice-start
  119.2 175.2 %collective-permute-start.7 = (bf16[6,32,32,128]{3,2,1,0:T(8,128)(2,1)S(1)}, bf16[6,32,32,128]{3,2,1,0:T(8,128)(2,1)S(1)}, u32[]{:S(2)}, u32[]{:S(2)}) collective-permute-start(bf16[6,32,32,128]{3,2,1,0:T(8,128)(2,1)S(1)} %copy-done.59), channel_id=1, source_target_pairs={{3,0},{4,1},{5,2},{6,3},{7,4},{0,5},{1,6},{2,7},{11,8},{12,9},{13,... | collective-permute-start | bytes 4718600 | tf_op jit(solution)/shard_map/ppermute | solution.py:15
  127.3 287.8 %collective-permute-start.8 = (bf16[6,32,32,128]{3,2,1,0:T(8,128)(2,1)S(1)}, bf16[6,32,32,128]{3,2,1,0:T(8,128)(2,1)S(1)}, u32[]{:S(2)}, u32[]{:S(2)}) collective-permute-start(bf16[6,32,32,128]{3,2,1,0:T(8,128)(2,1)S(1)} %copy-done.61), channel_id=1, source_target_pairs={{5,0},{6,1},{7,2},{0,3},{1,4},{2,5},{3,6},{4,7},{13,8},{14,9},{15,... | collective-permute-start | bytes 4718600 | tf_op jit(solution)/shard_map/ppermute | solution.py:15
  131.2 115.1 %copy-start.52 = (bf16[6,33,32,128]{3,2,1,0:T(8,128)(2,1)S(1)}, bf16[6,33,32,128]{3,2,1,0:T(8,128)(2,1)}, u32[]{:S(2)}) copy-start(bf16[6,33,32,128]{3,2,1,0:T(8,128)(2,1)} %slice.879) | copy-start | bytes 4866052
  131.2 147.9 %copy-start.60 = (bf16[6,32,32,128]{3,2,1,0:T(8,128)(2,1)S(1)}, bf16[6,32,32,128]{3,2,1,0:T(8,128)(2,1)}, u32[]{:S(2)}) copy-start(bf16[6,32,32,128]{3,2,1,0:T(8,128)(2,1)} %get-tuple-element.130) | copy-start | bytes 4718596
  246.3 269.5 %collective-permute-start.4 = (bf16[6,33,32,128]{3,2,1,0:T(8,128)(2,1)S(1)}, bf16[6,33,32,128]{3,2,1,0:T(8,128)(2,1)S(1)}, u32[]{:S(2)}, u32[]{:S(2)}) collective-permute-start(bf16[6,33,32,128]{3,2,1,0:T(8,128)(2,1)S(1)} %copy-done.52), channel_id=1, source_target_pairs={{5,0},{6,1},{7,2},{0,3},{1,4},{2,5},{3,6},{4,7},{13,8},{14,9},{15,... | collective-permute-start | bytes 4866056 | tf_op jit(solution)/shard_map/ppermute | solution.py:15
  279.1 235.5 %collective-permute-start.9 = (bf16[6,32,32,128]{3,2,1,0:T(8,128)(2,1)S(1)}, bf16[6,32,32,128]{3,2,1,0:T(8,128)(2,1)S(1)}, u32[]{:S(2)}, u32[]{:S(2)}) collective-permute-start(bf16[6,32,32,128]{3,2,1,0:T(8,128)(2,1)S(1)} %copy-done.60), channel_id=1, source_target_pairs={{6,0},{7,1},{0,2},{1,3},{2,4},{3,5},{4,6},{5,7},{14,8},{15,9},{8,1... | collective-permute-start | bytes 4718600 | tf_op jit(solution)/shard_map/ppermute | solution.py:15
  287.5 329.4 %collective-permute-start.5 = (bf16[6,31,32,128]{3,2,1,0:T(8,128)(2,1)}, bf16[6,31,32,128]{3,2,1,0:T(8,128)(2,1)}, u32[]{:S(2)}, u32[]{:S(2)}) collective-permute-start(bf16[6,31,32,128]{3,2,1,0:T(8,128)(2,1)} %slice.880), channel_id=1, source_target_pairs={{6,0},{7,1},{0,2},{1,3},{2,4},{3,5},{4,6},{5,7},{14,8},{15,9},{8,1... | collective-permute-start | bytes 4571144 | tf_op jit(solution)/shard_map/ppermute | solution.py:15
  294.4 122.6 %copy-start.53 = (bf16[6,32,32,128]{3,2,1,0:T(8,128)(2,1)}, bf16[6,32,32,128]{3,2,1,0:T(8,128)(2,1)S(1)}, u32[]{:S(2)}) copy-start(bf16[6,32,32,128]{3,2,1,0:T(8,128)(2,1)S(1)} %collective-permute-done.7) | copy-start | bytes 4718596
  294.4 357.3 %collective-permute-start.2 = (bf16[6,33,32,128]{3,2,1,0:T(8,128)(2,1)S(1)}, bf16[6,33,32,128]{3,2,1,0:T(8,128)(2,1)}, u32[]{:S(2)}, u32[]{:S(2)}) collective-permute-start(bf16[6,33,32,128]{3,2,1,0:T(8,128)(2,1)S(1)} %slice.876), channel_id=1, source_target_pairs={{2,0},{3,1},{4,2},{5,3},{6,4},{7,5},{0,6},{1,7},{10,8},{11,9},{12,... | collective-permute-start | bytes 4866056 | tf_op jit(solution)/shard_map/ppermute | solution.py:15
  415.1 238.4 %collective-permute-start.3 = (bf16[6,31,32,128]{3,2,1,0:T(8,128)(2,1)}, bf16[6,31,32,128]{3,2,1,0:T(8,128)(2,1)}, u32[]{:S(2)}, u32[]{:S(2)}) collective-permute-start(bf16[6,31,32,128]{3,2,1,0:T(8,128)(2,1)} %slice.877), channel_id=1, source_target_pairs={{3,0},{4,1},{5,2},{6,3},{7,4},{0,5},{1,6},{2,7},{11,8},{12,9},{13,... | collective-permute-start | bytes 4571144 | tf_op jit(solution)/shard_map/ppermute | solution.py:15
  514.7 140.6 %collective-permute-start.11 = (bf16[6,33,32,128]{3,2,1,0:T(8,128)(2,1)S(1)}, bf16[6,33,32,128]{3,2,1,0:T(8,128)(2,1)S(1)}, u32[]{:S(2)}, u32[]{:S(2)}) collective-permute-start(bf16[6,33,32,128]{3,2,1,0:T(8,128)(2,1)S(1)} %slice.923), channel_id=1, source_target_pairs={{3,0},{4,1},{5,2},{6,3},{7,4},{0,5},{1,6},{2,7},{11,8},{12,9},{13,... | collective-permute-start | bytes 4866056 | tf_op jit(solution)/shard_map/ppermute | solution.py:15
  515.8 170.6 %collective-permute-start.13 = (bf16[6,33,32,128]{3,2,1,0:T(8,128)(2,1)S(1)}, bf16[6,33,32,128]{3,2,1,0:T(8,128)(2,1)S(1)}, u32[]{:S(2)}, u32[]{:S(2)}) collective-permute-start(bf16[6,33,32,128]{3,2,1,0:T(8,128)(2,1)S(1)} %slice.928), channel_id=1, source_target_pairs={{6,0},{7,1},{0,2},{1,3},{2,4},{3,5},{4,6},{5,7},{14,8},{15,9},{8,1... | collective-permute-start | bytes 4866056 | tf_op jit(solution)/shard_map/ppermute | solution.py:15
  961.7 13.3 copy-start.69
  961.7 13.3 copy-start.70
  983.0 13.8 slice-start.2
  988.5 15.7 slice-start.4
  1049.1 457.5 %copy-start.71 = (f32[13,64]{1,0:T(8,128)S(1)}, f32[13,64]{1,0:T(8,128)}, u32[]{:S(2)}) copy-start(f32[13,64]{1,0:T(8,128)} %get-tuple-element.208) | copy-start | bytes 9988
  1049.2 1068.5 %reduce-scatter.5.cloned.1.call-start = ((), (), s32[]{:S(2)}) async-start(), calls=%async_computation.5 | async-start | bytes 34078720 | tf_op jit(solution)/shard_map/reduce_scatter | solution.py:121
  1742.0 10.4 copy-start.49
  1756.1 9.8 copy-start.34
  1879.3 238.4 %copy-start.72 = (f32[13,64]{1,0:T(8,128)S(1)}, f32[13,64]{1,0:T(8,128)}, u32[]{:S(2)}) copy-start(f32[13,64]{1,0:T(8,128)} %get-tuple-element.208) | copy-start | bytes 9988
  (70 other events, 337.6 us)
Sparse Core Ops, SparseCore 0:
  1049.3 457.2 reduce-scatter.2
  1879.5 238.1 reduce-scatter.4
